TPU v7x, 512 devices: a whole 4x8x8 slice. The times are simulated.
512 devices in a mesh: mem: 8 (over z_lo, core), space: 64 (over z_hi, x, y).
Axes of the slice: x: 4, y: 8, z: 8 (z_hi: 2, z_lo: 4; z = z_hi * 4 + z_lo), core: 2. Of those that a mesh axis runs over, the one named last changes fastest.
Arguments:
- log_perm: float32 [128, 128, 2048], P('space', 'mem'), may hold values from -2 to 2
- concentration: float32 [128, 128, 2048], P('space', 'mem'), may hold values from -6 to 6
- well_cells: int32 [128], replicated, may hold values from 0 to 262143
- obs_data: float32 [128], replicated, may hold values from -6 to 6
- obs_var: float32 [128], replicated, may hold values from 0.05 to 0.5
- obs_noise: float32 [128, 128], P('mem'), may hold values from -6 to 6
Outputs:
- forecast: float32 [128, 128, 2048], P('space', 'mem')
- updated_log_perm: float32 [128, 128, 2048], P('space', 'mem')
Inputs may be any that keep to these rules, and one draw needn't show every extreme that they name: `well_cells`: cells flattened as row times 2048 plus column.
All inputs are finite; a program needn't handle non-finite values.
Results may differ from a plain program's by a relative error of at most 0.0034.
Values may be sent and summed in bfloat16 or wider, within the bound.
No kernel may reach another device: no remote copies, remote signals or barrier semaphores. Data moves between devices by JAX's collectives and lax.ppermute only.
A program may use at most 128 MiB of HBM per device.

v0:
```python
import jax
import jax.numpy as jnp
from jax import lax
from jax.sharding import PartitionSpec as P

time_step = 0.03
inflation = 4.0


def with_halo(block, sides, width):
    for axis, dim in sides:
        count = lax.axis_size(axis)
        forward = [(i, i + 1) for i in range(count - 1)]
        backward = [(target, source) for source, target in forward]
        low = lax.ppermute(
            lax.slice_in_dim(block, block.shape[dim] - width, None, axis=dim), axis, forward
        )
        high = lax.ppermute(lax.slice_in_dim(block, 0, width, axis=dim), axis, backward)
        block = jnp.concatenate([low, block, high], axis=dim)
    return block


def advance(conc_ext, conduct_ext):
    conc_pad = jnp.pad(conc_ext, ((0, 0), (0, 0), (1, 1)))
    cond_pad = jnp.pad(conduct_ext, ((0, 0), (0, 0), (1, 1)))
    centre = conc_pad[1:-1, :, 1:-1]
    centre_cond = cond_pad[1:-1, :, 1:-1]
    inflow = jnp.zeros_like(centre)
    sides = (
        (conc_pad[:-2, :, 1:-1], cond_pad[:-2, :, 1:-1]),
        (conc_pad[2:, :, 1:-1], cond_pad[2:, :, 1:-1]),
        (conc_pad[1:-1, :, :-2], cond_pad[1:-1, :, :-2]),
        (conc_pad[1:-1, :, 2:], cond_pad[1:-1, :, 2:]),
    )
    for conc_side, cond_side in sides:
        inflow = inflow + 0.5 * (centre_cond + cond_side) * (conc_side - centre)
    return centre + time_step * inflow


def cholesky_solve(matrix, target):
    factor = jnp.linalg.cholesky(matrix)
    middle = lax.linalg.triangular_solve(factor, target, left_side=True, lower=True)
    return lax.linalg.triangular_solve(factor, middle, left_side=True, lower=True, transpose_a=True)


def transform(predicted, noise_all, obs_data, obs_var):
    members = predicted.shape[0]
    anomaly = predicted - jnp.mean(predicted, axis=0, keepdims=True)
    covariance = jnp.dot(
        anomaly.T, anomaly, precision=lax.Precision.HIGHEST, preferred_element_type=jnp.float32
    ) / (members - 1) + inflation * jnp.diag(obs_var)
    innovation = obs_data[None, :] + jnp.sqrt(inflation * obs_var)[None, :] * noise_all - predicted
    solved = cholesky_solve(covariance, innovation.T)
    weights = jnp.dot(
        anomaly, solved, precision=lax.Precision.HIGHEST, preferred_element_type=jnp.float32
    ) / (members - 1)
    centred = weights - jnp.mean(weights, axis=0, keepdims=True)
    return centred.astype(jnp.bfloat16)


def local(log_perm, concentration, well_cells, obs_data, obs_var, obs_noise):
    row_count, member_dev, col_count = log_perm.shape
    tile_index = lax.axis_index("space")
    group_index = lax.axis_index("mem")
    conduct = jnp.exp(log_perm)
    tracer = concentration
    for repeat in range(2):
        padded = with_halo(jnp.stack([tracer, conduct]), (("space", 1),), 1)
        tracer = advance(padded[0], padded[1])
    first_cell = tile_index * (row_count * col_count)
    local_cell = well_cells - first_cell
    inside_tile = (local_cell >= 0) & (local_cell < row_count * col_count)
    clipped = jnp.clip(local_cell, 0, row_count * col_count - 1)
    picked = tracer[clipped // col_count, :, clipped % col_count]
    picked = jnp.where(inside_tile[:, None], picked, 0.0).T
    summed = lax.psum(picked, "space")
    predicted, noise_all = (
        lax.all_gather(summed, "mem", axis=0, tiled=True),
        lax.all_gather(obs_noise, "mem", axis=0, tiled=True),
    )
    centred = transform(predicted, noise_all, obs_data, obs_var)
    perm_low = log_perm.astype(jnp.bfloat16)
    my_columns = lax.dynamic_slice_in_dim(centred, group_index * member_dev, member_dev, 1)
    increment = jnp.einsum(
        "xiy,ij->xjy",
        lax.all_gather(perm_low, "mem", axis=1, tiled=True),
        my_columns,
        preferred_element_type=jnp.float32,
    )
    return (tracer, log_perm + increment)


def solution(mesh):
    return jax.shard_map(
        local,
        mesh=mesh,
        in_specs=(P("space", "mem", None), P("space", "mem", None), P(), P(), P(), P("mem", None)),
        out_specs=(P("space", "mem", None), P("space", "mem", None)),
        check_vma=False,
    )
```

profile of v0, /device:TPU:257, one launch (start us, length us, event | category | flops | bytes accessed | tf_op | source)
XLA Modules:
  0.0 546.4 jit_solution(17036058877172273697)
XLA Ops:
  7.2 1.0 exponential_bitcast_fusion
  8.2 1.0 fusion.10
  9.2 3.7 collective-permute-start.1
  12.9 1.9 collective-permute-start
  14.8 0.7 fusion.75
  15.5 2.8 collective-permute-done.1
  18.3 13.8 %collective-permute-done = f32[2,1,16,2048]{3,2,1,0:T(8,128)S(1)} collective-permute-done((f32[2,1,16,2048]{3,2,1,0:T(8,128)S(1)}, f32[2,1,16,2048]{3,2,1,0:T(8,128)S(1)}, u32[]{:S(2)}, u32[]{:S(2)}) %collective-permute-start) | collective-permute-done | bytes 262176 | tf_op jit(solution)/shard_map/ppermute | solution.py:15
  32.1 1.0 fusion.2
  33.2 0.2 fusion.7
  33.5 0.6 copy-done.1
  34.1 0.9 fusion.79
  35.1 1.9 collective-permute-start.3
  37.0 3.4 collective-permute-start.2
  40.4 19.5 %all_gather.10 = f32[128,128]{1,0:T(8,128)S(1)} all-gather(f32[16,128]{1,0:T(8,128)S(1)} %copy-done.3), channel_id=1, replica_groups=mesh['mem'=8,'space'=64] {'mem'}, dimensions={0}, use_global_device_ids=true | all-gather | bytes 73728 | tf_op jit(solution)/shard_map/all_gather | solution.py:79
  60.1 0.2 fusion.8
  60.3 0.4 fusion.29
  60.7 0.6 copy.44
  61.3 1.2 gather_fusion
  62.5 0.1 select_bitcast_fusion
  62.6 381.0 %psum.7 = f32[16,128]{0,1:T(8,128)S(1)} all-reduce(f32[16,128]{0,1:T(8,128)S(1)} %select_bitcast_fusion), channel_id=1, replica_groups=mesh['mem'=8,'space'=64] {'space'}, use_global_device_ids=true, to_apply=%region_0.1 | all-reduce | flops 2048 | bytes 16384 | tf_op jit(solution)/shard_map/psum | solution.py:76
  443.7 69.2 %all_gather.9 = f32[128,128]{1,0:T(8,128)S(1)} all-gather(f32[16,128]{1,0:T(8,128)S(1)} %copy.45), channel_id=1, replica_groups=mesh['mem'=8,'space'=64] {'mem'}, dimensions={0}, use_global_device_ids=true | all-gather | bytes 73728 | tf_op jit(solution)/shard_map/all_gather | solution.py:78
  512.9 0.3 convolution_multiply_fusion.1
  513.2 0.1 copy.47
  513.3 0.1 fusion.59
  513.4 11.7 %cholesky.16 = f32[128,128]{1,0:T(8,128)S(1)} custom-call(f32[128,128]{1,0:T(8,128)S(1)} %fusion.59), custom_call_target="Cholesky" | custom-call | tf_op jit(solution)/shard_map/jit(cholesky)/cholesky | solution.py:41
  525.1 0.7 compare_reduce_fusion
  525.8 0.6 fusion.53
  526.5 9.8 %custom-call.8 = f32[1,128,128]{1,2,0:T(8,128)S(1)} custom-call(f32[1,128,128]{2,1,0:T(8,128)S(1)} %fusion.53), custom_call_target="InvertDiagBlocksLowerTriangular" | custom-call | tf_op jit(solution)/shard_map/triangular_solve | solution.py:43
  536.3 0.3 fusion.56
  536.6 0.2 fusion.54
  536.8 0.4 fusion.80
  537.3 2.2 fusion
  (30 shorter events, 0.6 us)
Async XLA Ops:
  7.2 530.1 %all-gather.2.cloned.1.call-start = ((), (), s32[]{:S(2)}) async-start(), calls=%async_computation | async-start | bytes 1179648 | tf_op jit(solution)/shard_map/all_gather | solution.py:86
  9.2 9.1 %collective-permute-start.1 = (f32[2,1,16,2048]{3,2,1,0:T(8,128)S(1)}, f32[2,1,16,2048]{3,2,1,0:T(8,128)S(1)}, u32[]{:S(2)}, u32[]{:S(2)}) collective-permute-start(f32[2,1,16,2048]{3,2,1,0:T(8,128)S(1)} %get-tuple-element.17), channel_id=1, source_target_pairs={{1,0},{2,1},{3,2},{4,3},{5,4},{6,5},{7,6},{8,7},{9,8},{10,9},{11,1... | collective-permute-start | bytes 786440 | tf_op jit(solution)/shard_map/ppermute | solution.py:18
  12.9 19.2 %collective-permute-start = (f32[2,1,16,2048]{3,2,1,0:T(8,128)S(1)}, f32[2,1,16,2048]{3,2,1,0:T(8,128)S(1)}, u32[]{:S(2)}, u32[]{:S(2)}) collective-permute-start(f32[2,1,16,2048]{3,2,1,0:T(8,128)S(1)} %get-tuple-element.16), channel_id=1, source_target_pairs={{0,1},{1,2},{2,3},{3,4},{4,5},{5,6},{6,7},{7,8},{8,9},{9,10},{10,1... | collective-permute-start | bytes 786440 | tf_op jit(solution)/shard_map/ppermute | solution.py:15
  15.5 17.8 %copy-start = (f32[2,16,2048]{2,1,0:T(8,128)S(1)}, f32[2,16,2048]{2,1,0:T(8,128)}, u32[]{:S(2)}) copy-start(f32[2,16,2048]{2,1,0:T(8,128)} %param.7) | copy-start | bytes 786436
  33.1 1.0 copy-start.1
  33.4 7.0 %copy-start.6 = (s32[128]{0:T(128)S(1)}, s32[128]{0:T(128)}, u32[]{:S(2)}) copy-start(s32[128]{0:T(128)} %param.8) | copy-start | bytes 1540
  33.4 7.0 %copy-start.3 = (f32[16,128]{1,0:T(8,128)S(1)}, f32[16,128]{1,0:T(8,128)}, u32[]{:S(2)}) copy-start(f32[16,128]{1,0:T(8,128)} %param.11) | copy-start | bytes 24580
  33.5 26.4 %copy-start.4 = (f32[128]{0:T(128)S(1)}, f32[128]{0:T(128)}, u32[]{:S(2)}) copy-start(f32[128]{0:T(128)} %param.10) | copy-start | bytes 1540
  35.1 24.9 %collective-permute-start.3 = (f32[2,1,16,2048]{3,2,1,0:T(8,128)S(1)}, f32[2,1,16,2048]{3,2,1,0:T(8,128)S(1)}, u32[]{:S(2)}, u32[]{:S(2)}) collective-permute-start(f32[2,1,16,2048]{3,2,1,0:T(8,128)S(1)} %get-tuple-element.13), channel_id=1, source_target_pairs={{1,0},{2,1},{3,2},{4,3},{5,4},{6,5},{7,6},{8,7},{9,8},{10,9},{11,1... | collective-permute-start | bytes 786440 | tf_op jit(solution)/shard_map/ppermute | solution.py:18
  37.0 22.9 %collective-permute-start.2 = (f32[2,1,16,2048]{3,2,1,0:T(8,128)S(1)}, f32[2,1,16,2048]{3,2,1,0:T(8,128)S(1)}, u32[]{:S(2)}, u32[]{:S(2)}) collective-permute-start(f32[2,1,16,2048]{3,2,1,0:T(8,128)S(1)} %get-tuple-element.12), channel_id=1, source_target_pairs={{0,1},{1,2},{2,3},{3,4},{4,5},{5,6},{6,7},{7,8},{8,9},{9,10},{10,1... | collective-permute-start | bytes 786440 | tf_op jit(solution)/shard_map/ppermute | solution.py:15
  60.7 475.9 %copy-start.2 = (f32[2,16,2048]{2,1,0:T(8,128)}, f32[2,16,2048]{2,1,0:T(8,128)S(1)}, u32[]{:S(2)}) copy-start(f32[2,16,2048]{2,1,0:T(8,128)S(1)} %fusion.29) | copy-start | bytes 786436
  60.7 475.6 %copy-start.5 = (f32[128]{0:T(128)S(1)}, f32[128]{0:T(128)}, u32[]{:S(2)}) copy-start(f32[128]{0:T(128)} %param.9) | copy-start | bytes 1540
Sparse Core Ops, SparseCore 0:
  60.1 35.0 all-gather.1
where the time goes:
time: 547 us; the launch traced here: 546 us
  blocking collectives  470 us (86%)
  other arithmetic  27.6 us (5%)
  waiting for transfers between devices  16.6 us (3%)
  between operations  14.3 us (3%)
  starting transfers between devices  10.9 us (2%)
    psum x1, blocking collectives, local(): summed = lax.psum(picked, 'space')  381 us
    all_gather x1, blocking collectives, local(): lax.all_gather(summed, 'mem', axis=0, tiled=True)  69.2 us
    all_gather x1, blocking collectives, local(): lax.all_gather(obs_noise, 'mem', axis=0, tiled=True)  19.5 us
    ppermute x2, waiting for transfers between devices, with_halo(): lax.ppermute(lax.slice_in_dim(block, block.shape[dim] - width, None, axis...  13.8 us
    another operation x3, other arithmetic, cholesky_solve(): factor = jnp.linalg.cholesky(matrix)  12.4 us
  transfers between devices with their start and end apart: 5, of which 2 were waited for; matrix products, arithmetic and copies ran while one was open for 5% of the time, Pallas kernels for 0%

commit v1 on v0

--- a/solution.py
+++ b/solution.py
@@ -73,7 +73,8 @@
     clipped = jnp.clip(local_cell, 0, row_count * col_count - 1)
     picked = tracer[clipped // col_count, :, clipped % col_count]
     picked = jnp.where(inside_tile[:, None], picked, 0.0).T
-    summed = lax.psum(picked, "space")
+    blocks = lax.all_gather(picked, "space")
+    summed = jnp.sum(blocks, axis=0)
     predicted, noise_all = (
         lax.all_gather(summed, "mem", axis=0, tiled=True),
         lax.all_gather(obs_noise, "mem", axis=0, tiled=True),

time: 547 us -> 334 us (0.61)
  blocking collectives: 470 us -> 257 us
    psum x1 -> x0, blocking collectives: 381 us -> none  [local(): summed = lax.psum(picked, 'space')]
    all_gather x0 -> x1, blocking collectives: none -> 196 us  [local(): blocks = lax.all_gather(picked, 'space')]
    all_gather x1, blocking collectives: 69.2 us -> 41.5 us  [local(): lax.all_gather(summed, 'mem', axis=0, tiled=True)]
  transfers between devices with their start and end apart: 5 -> 5, of which waited for: 2 -> 2; matrix products, arithmetic and copies ran while one was open for 5% -> 8% of each run, Pallas kernels for 0% -> 0%
where the time goes in v1:
time: 334 us
  blocking collectives  257 us (77%)
  other arithmetic  27.7 us (8%)
  waiting for transfers between devices  16.6 us (5%)
  between operations  14.3 us (4%)
  starting transfers between devices  10.9 us (3%)
  local copies, waits for them, and re-layouts  3.87 us (1%)
  matrix products  3.39 us (1%)
    all_gather x1, blocking collectives, local(): blocks = lax.all_gather(picked, 'space')  196 us
    all_gather x1, blocking collectives, local(): lax.all_gather(summed, 'mem', axis=0, tiled=True)  41.5 us
    all_gather x1, blocking collectives, local(): lax.all_gather(obs_noise, 'mem', axis=0, tiled=True)  19.5 us
    ppermute x2, waiting for transfers between devices, with_halo(): lax.ppermute(lax.slice_in_dim(block, block.shape[dim] - width, None, axis...  13.8 us
    another operation x3, other arithmetic, cholesky_solve(): factor = jnp.linalg.cholesky(matrix)  12.4 us
    another operation x2, other arithmetic, cholesky_solve(): lax.linalg.triangular_solve(factor, middle, left_side=True, lower=True, t...  10.4 us
  transfers between devices with their start and end apart: 5, of which 2 were waited for; matrix products, arithmetic and copies ran while one was open for 8% of the time, Pallas kernels for 0%

profile of v1, /device:TPU:257, one launch (start us, length us, event | category | flops | bytes accessed | tf_op | source)
XLA Modules:
  0.0 333.8 jit_solution(12880356906473842103)
XLA Ops:
  7.2 1.0 exponential_bitcast_fusion
  8.2 1.0 fusion.10
  9.2 3.7 %collective-permute-start.1 = (f32[2,1,16,2048]{3,2,1,0:T(8,128)S(1)}, f32[2,1,16,2048]{3,2,1,0:T(8,128)S(1)}, u32[]{:S(2)}, u32[]{:S(2)}) collective-permute-start(f32[2,1,16,2048]{3,2,1,0:T(8,128)S(1)} %get-tuple-element.19), channel_id=1, source_target_pairs={{1,0},{2,1},{3,2},{4,3},{5,4},{6,5},{7,6},{8,7},{9,8},{10,9},{11,1... | collective-permute-start | bytes 786440 | tf_op jit(solution)/shard_map/ppermute | solution.py:18
  12.9 1.9 collective-permute-start
  14.8 0.7 fusion.75
  15.5 2.8 collective-permute-done.1
  18.3 13.8 %collective-permute-done = f32[2,1,16,2048]{3,2,1,0:T(8,128)S(1)} collective-permute-done((f32[2,1,16,2048]{3,2,1,0:T(8,128)S(1)}, f32[2,1,16,2048]{3,2,1,0:T(8,128)S(1)}, u32[]{:S(2)}, u32[]{:S(2)}) %collective-permute-start) | collective-permute-done | bytes 262176 | tf_op jit(solution)/shard_map/ppermute | solution.py:15
  32.1 1.0 fusion.2
  33.2 0.2 fusion.7
  33.5 0.6 copy-done.1
  34.1 0.9 fusion.79
  35.1 1.9 collective-permute-start.3
  37.0 3.4 %collective-permute-start.2 = (f32[2,1,16,2048]{3,2,1,0:T(8,128)S(1)}, f32[2,1,16,2048]{3,2,1,0:T(8,128)S(1)}, u32[]{:S(2)}, u32[]{:S(2)}) collective-permute-start(f32[2,1,16,2048]{3,2,1,0:T(8,128)S(1)} %get-tuple-element.14), channel_id=1, source_target_pairs={{0,1},{1,2},{2,3},{3,4},{4,5},{5,6},{6,7},{7,8},{8,9},{9,10},{10,1... | collective-permute-start | bytes 786440 | tf_op jit(solution)/shard_map/ppermute | solution.py:15
  40.4 19.5 %all_gather.18 = f32[128,128]{1,0:T(8,128)S(1)} all-gather(f32[16,128]{1,0:T(8,128)S(1)} %copy-done.3), channel_id=1, replica_groups=mesh['mem'=8,'space'=64] {'mem'}, dimensions={0}, use_global_device_ids=true | all-gather | bytes 73728 | tf_op jit(solution)/shard_map/all_gather | solution.py:80
  60.1 0.2 fusion.8
  60.3 0.4 fusion.29
  60.7 0.6 copy.54
  61.3 1.2 gather_fusion
  62.5 0.1 select_bitcast_fusion
  62.7 196.1 %all-gather = f32[1024,128]{1,0:T(8,128)S(1)} all-gather(f32[16,128]{1,0:T(8,128)S(1)} %copy.55), channel_id=2, replica_groups=mesh['mem'=8,'space'=64] {'space'}, dimensions={0}, use_global_device_ids=true | all-gather | bytes 532480 | tf_op jit(solution)/shard_map/all_gather | solution.py:76
  258.8 41.5 %all_gather.17 = f32[128,128]{1,0:T(8,128)S(1)} all-gather(f32[16,128]{1,0:T(8,128)S(1)} %reduce_sum.27), channel_id=1, replica_groups=mesh['mem'=8,'space'=64] {'mem'}, dimensions={0}, use_global_device_ids=true | all-gather | bytes 73728 | tf_op jit(solution)/shard_map/all_gather | solution.py:79
  300.3 0.3 convolution_multiply_fusion.1
  300.6 0.1 copy.57
  300.7 0.1 fusion.59
  300.8 11.7 %cholesky.16 = f32[128,128]{1,0:T(8,128)S(1)} custom-call(f32[128,128]{1,0:T(8,128)S(1)} %fusion.59), custom_call_target="Cholesky" | custom-call | tf_op jit(solution)/shard_map/jit(cholesky)/cholesky | solution.py:41
  312.6 0.7 compare_reduce_fusion
  313.3 0.6 fusion.53
  313.9 9.8 %custom-call.8 = f32[1,128,128]{1,2,0:T(8,128)S(1)} custom-call(f32[1,128,128]{2,1,0:T(8,128)S(1)} %fusion.53), custom_call_target="InvertDiagBlocksLowerTriangular" | custom-call | tf_op jit(solution)/shard_map/triangular_solve | solution.py:43
  323.7 0.3 fusion.56
  324.0 0.2 fusion.54
  324.2 0.4 fusion.80
  324.7 2.2 fusion
  (31 shorter events, 0.7 us)
Async XLA Ops:
  7.2 317.5 %all-gather.3.cloned.1.call-start = ((), (), s32[]{:S(2)}) async-start(), calls=%async_computation | async-start | bytes 1179648 | tf_op jit(solution)/shard_map/all_gather | solution.py:87
  9.2 9.1 %collective-permute-start.1 = (f32[2,1,16,2048]{3,2,1,0:T(8,128)S(1)}, f32[2,1,16,2048]{3,2,1,0:T(8,128)S(1)}, u32[]{:S(2)}, u32[]{:S(2)}) collective-permute-start(f32[2,1,16,2048]{3,2,1,0:T(8,128)S(1)} %get-tuple-element.19), channel_id=1, source_target_pairs={{1,0},{2,1},{3,2},{4,3},{5,4},{6,5},{7,6},{8,7},{9,8},{10,9},{11,1... | collective-permute-start | bytes 786440 | tf_op jit(solution)/shard_map/ppermute | solution.py:18
  12.9 19.2 %collective-permute-start = (f32[2,1,16,2048]{3,2,1,0:T(8,128)S(1)}, f32[2,1,16,2048]{3,2,1,0:T(8,128)S(1)}, u32[]{:S(2)}, u32[]{:S(2)}) collective-permute-start(f32[2,1,16,2048]{3,2,1,0:T(8,128)S(1)} %get-tuple-element.18), channel_id=1, source_target_pairs={{0,1},{1,2},{2,3},{3,4},{4,5},{5,6},{6,7},{7,8},{8,9},{9,10},{10,1... | collective-permute-start | bytes 786440 | tf_op jit(solution)/shard_map/ppermute | solution.py:15
  15.5 17.8 %copy-start = (f32[2,16,2048]{2,1,0:T(8,128)S(1)}, f32[2,16,2048]{2,1,0:T(8,128)}, u32[]{:S(2)}) copy-start(f32[2,16,2048]{2,1,0:T(8,128)} %param.7) | copy-start | bytes 786436
  33.1 1.0 copy-start.1
  33.4 7.0 %copy-start.6 = (s32[128]{0:T(128)S(1)}, s32[128]{0:T(128)}, u32[]{:S(2)}) copy-start(s32[128]{0:T(128)} %param.8) | copy-start | bytes 1540
  33.4 7.0 %copy-start.3 = (f32[16,128]{1,0:T(8,128)S(1)}, f32[16,128]{1,0:T(8,128)}, u32[]{:S(2)}) copy-start(f32[16,128]{1,0:T(8,128)} %param.11) | copy-start | bytes 24580
  33.5 26.4 %copy-start.4 = (f32[128]{0:T(128)S(1)}, f32[128]{0:T(128)}, u32[]{:S(2)}) copy-start(f32[128]{0:T(128)} %param.10) | copy-start | bytes 1540
  35.1 24.9 %collective-permute-start.3 = (f32[2,1,16,2048]{3,2,1,0:T(8,128)S(1)}, f32[2,1,16,2048]{3,2,1,0:T(8,128)S(1)}, u32[]{:S(2)}, u32[]{:S(2)}) collective-permute-start(f32[2,1,16,2048]{3,2,1,0:T(8,128)S(1)} %get-tuple-element.15), channel_id=1, source_target_pairs={{1,0},{2,1},{3,2},{4,3},{5,4},{6,5},{7,6},{8,7},{9,8},{10,9},{11,1... | collective-permute-start | bytes 786440 | tf_op jit(solution)/shard_map/ppermute | solution.py:18
  37.0 22.9 %collective-permute-start.2 = (f32[2,1,16,2048]{3,2,1,0:T(8,128)S(1)}, f32[2,1,16,2048]{3,2,1,0:T(8,128)S(1)}, u32[]{:S(2)}, u32[]{:S(2)}) collective-permute-start(f32[2,1,16,2048]{3,2,1,0:T(8,128)S(1)} %get-tuple-element.14), channel_id=1, source_target_pairs={{0,1},{1,2},{2,3},{3,4},{4,5},{5,6},{6,7},{7,8},{8,9},{9,10},{10,1... | collective-permute-start | bytes 786440 | tf_op jit(solution)/shard_map/ppermute | solution.py:15
  60.7 198.1 %copy-start.2 = (f32[2,16,2048]{2,1,0:T(8,128)}, f32[2,16,2048]{2,1,0:T(8,128)S(1)}, u32[]{:S(2)}) copy-start(f32[2,16,2048]{2,1,0:T(8,128)S(1)} %fusion.29) | copy-start | bytes 786436
  60.7 263.0 %copy-start.5 = (f32[128]{0:T(128)S(1)}, f32[128]{0:T(128)}, u32[]{:S(2)}) copy-start(f32[128]{0:T(128)} %param.9) | copy-start | bytes 1540
Sparse Core Ops, SparseCore 0:
  60.1 35.0 all-gather.2
